TPU v7x, 512 devices: a whole 4x4x16 slice. The times are simulated.
512 devices in a mesh: gz: 16 (over y, x), pa: 32 (over z, core).
Axes of the slice: x: 4, y: 4, z: 16, core: 2. Of those that a mesh axis runs over, the one named last changes fastest.
Arguments:
- particles: float32 [6, 1048576], P(None, ('gz', 'pa')), may hold values from -6 to 6
- slice_index: int32 [1048576], P(('gz', 'pa')), may hold values from 0 to 127
- moving: int32 [16, 32, 2], P('gz', 'pa'), may hold values from 0 to 384, as said below
- decay_rate: float32 [8], replicated, may hold values from 0.3 to 600
- wake_freq: float32 [8], replicated, may hold values from -3.140625 to 3.140625
- wake_amp: float32 [4, 8], replicated, may hold values from -3 to 3
Outputs:
- wake_kick: float32 [3, 2048], P(None, 'gz')
- particles_out: float32 [6, 1441792], P(None, ('gz', 'pa'))
Inputs may be any that keep to these rules, and one draw needn't show every extreme that they name: `moving`: each entry is at most 384, and some entry equals 384.
All inputs are finite; a program needn't handle non-finite values.
Results may differ from a plain program's by a relative error of at most 0.0003.
Values sent between devices are 32-bit elements; how exact they have to be, the bound alone decides.
No kernel may reach another device: no remote copies, remote signals or barrier semaphores. Data moves between devices by JAX's collectives and lax.ppermute only.
A program may use at most 64 MiB of HBM per device.

v0:
```python
import math
import jax
import jax.numpy as jnp
from jax import lax
from jax.sharding import PartitionSpec as P

S_DEV = 128
two_pi = 6.283185307179586
adjust_horiz = 0.269
adjust_vert = 0.355
chroma_horiz = 0.05
chroma_vert = 0.04
curve_horiz = 0.02
curve_vert = -0.015
detune_self = 0.03
detune_cross = -0.02
voltage = 0.05
synch_phase = 0.3
slippage = 0.1


def from_behind_2(value, axis, steps):
    count = lax.axis_size(axis)
    leading, last = (max(0, -steps), min(count, count - steps))
    return lax.ppermute(value, axis, [(source, source + steps) for source in range(leading, last)])


def complex_mul(first, second):
    return jnp.stack(
        [first[0] * second[0] - first[1] * second[1], first[0] * second[1] + first[1] * second[0]]
    )


def powers(damping, wake_freq, distance):
    envelope = jnp.exp(-damping[:, None] * distance[None, :])
    angles = wake_freq[:, None] * distance[None, :]
    return (envelope * jnp.cos(angles), envelope * jnp.sin(angles))


def toeplitz(wave):
    slab_width = wave.shape[0]
    row_index = lax.broadcasted_iota(jnp.int32, (slab_width, slab_width), 0)
    col_index = lax.broadcasted_iota(jnp.int32, (slab_width, slab_width), 1)
    offset = col_index - row_index
    picked = jnp.take(wave, jnp.clip(offset, 0, slab_width - 1))
    return jnp.where(offset > 0, picked, jnp.float32(0.0))


def slab_tables(decay_rate, wake_freq, wake_amp, slab_width, slice_total):
    damping = decay_rate / slice_total
    norm_trans = jnp.sqrt(2.0 * damping)
    norm_long = jnp.sqrt(damping * damping + wake_freq * wake_freq)
    coef_real = jnp.stack(
        [wake_amp[0] * norm_trans, wake_amp[0] * norm_trans, wake_amp[2] * norm_long], axis=1
    )
    coef_imag = jnp.stack(
        [wake_amp[1] * norm_trans, wake_amp[1] * norm_trans, wake_amp[3] * norm_long], axis=1
    )
    distance = jnp.arange(slab_width, dtype=jnp.float32)
    near_re, near_im = powers(damping, wake_freq, distance)
    far_re, far_im = powers(damping, wake_freq, slab_width - distance)
    whole_re, whole_im = powers(damping, wake_freq, jnp.full((1,), slab_width, jnp.float32))
    factor = jnp.stack(
        [jnp.broadcast_to(whole_re, coef_real.shape), jnp.broadcast_to(whole_im, coef_real.shape)]
    )
    wave_trans = jnp.sum(
        norm_trans[:, None] * (wake_amp[0][:, None] * near_re - wake_amp[1][:, None] * near_im),
        axis=0,
    )
    wave_long = jnp.sum(
        norm_long[:, None] * (wake_amp[2][:, None] * near_re - wake_amp[3][:, None] * near_im),
        axis=0,
    )
    return (
        toeplitz(wave_trans),
        toeplitz(wave_long),
        near_re,
        near_im,
        far_re,
        far_im,
        factor,
        coef_real,
        coef_imag,
    )


def slab_summary(moments, tables):
    highest = lax.Precision.HIGHEST
    return jnp.stack(
        [
            jnp.dot(tables[4], moments.T, precision=highest),
            jnp.dot(tables[5], moments.T, precision=highest),
        ]
    )


def slab_kick(moments, carried, tables):
    highest = lax.Precision.HIGHEST
    trans_kick = jnp.dot(moments[0:2], tables[0], precision=highest)
    long_kick = jnp.dot(moments[2:3], tables[1], precision=highest)
    coef_re = tables[7] * carried[0] - tables[8] * carried[1]
    coef_im = tables[7] * carried[1] + tables[8] * carried[0]
    incoming = jnp.dot(coef_re.T, tables[2], precision=highest) - jnp.dot(
        coef_im.T, tables[3], precision=highest
    )
    return jnp.concatenate([trans_kick, long_kick], axis=0) + incoming


def moment_values(particles, mean_fill):
    root_fill = math.sqrt(mean_fill)
    return jnp.stack(
        [
            particles[0] / root_fill,
            particles[2] / root_fill,
            jnp.full_like(particles[0], 1.0 / mean_fill),
        ]
    )


def deposit(values, index, segments):
    return jax.vmap(lambda column: jax.ops.segment_sum(column, index, num_segments=segments))(
        values
    )


def one_turn(coords, kicks):
    hor_pos = coords[0]
    hor_mom = coords[1] + kicks[0]
    ver_pos = coords[2]
    ver_mom = coords[3] + kicks[1]
    lag_pos = coords[4]
    energy_dev = coords[5] + kicks[2]
    action_x = 0.5 * (hor_pos * hor_pos + hor_mom * hor_mom)
    action_y = 0.5 * (ver_pos * ver_pos + ver_mom * ver_mom)
    phase_x = two_pi * (
        adjust_horiz
        + chroma_horiz * energy_dev
        + curve_horiz * energy_dev * energy_dev
        + detune_self * action_x
        + detune_cross * action_y
    )
    phase_y = two_pi * (
        adjust_vert
        + chroma_vert * energy_dev
        + curve_vert * energy_dev * energy_dev
        + detune_self * action_y
        + detune_cross * action_x
    )
    cosine_x = jnp.cos(phase_x)
    sine_x = jnp.sin(phase_x)
    cosine_y = jnp.cos(phase_y)
    sine_y = jnp.sin(phase_y)
    new_energy = energy_dev - voltage * (jnp.sin(synch_phase + lag_pos) - math.sin(synch_phase))
    new_lag = lag_pos - slippage * new_energy
    return jnp.stack(
        [
            cosine_x * hor_pos + sine_x * hor_mom,
            cosine_x * hor_mom - sine_x * hor_pos,
            cosine_y * ver_pos + sine_y * ver_mom,
            cosine_y * ver_mom - sine_y * ver_pos,
            new_lag,
            new_energy,
        ]
    )


def upstream(own_summary, factor, slab_count):

    def advance(step_index, carried):
        return from_behind_2(complex_mul(factor, carried) + own_summary, "gz", 1)

    return lax.fori_loop(0, slab_count - 1, advance, jnp.zeros_like(own_summary))


def body(particles, slice_index, moving, decay_rate, wake_freq, wake_amp):
    slab_count = lax.axis_size("gz")
    member_count = lax.axis_size("pa")
    local_count = particles.shape[1]
    slab_width = S_DEV
    tables = slab_tables(decay_rate, wake_freq, wake_amp, slab_width, slab_width * slab_count)
    mean_fill = local_count * member_count / slab_width
    values = moment_values(particles, mean_fill)
    partial_moments = deposit(values, slice_index, slab_width)
    moments = lax.psum(partial_moments, "pa")
    carried = upstream(slab_summary(moments, tables), tables[6], slab_count)
    wake_kick = slab_kick(moments, carried, tables)
    per_particle = jnp.take(wake_kick, slice_index, axis=1)
    capacity = local_count * 3 // 16
    head_count = moving[0, 0, 0]
    tail_count = moving[0, 0, 1]
    slot_index = lax.broadcasted_iota(jnp.int32, (1, capacity), 1)
    leaving_head = slot_index < head_count
    leaving_tail = slot_index >= capacity - tail_count
    zero_value = jnp.float32(0.0)
    tail_start = local_count - capacity
    moved_all = one_turn(particles, per_particle)
    head_part = moved_all[:, :capacity]
    tail_part = moved_all[:, tail_start:]
    head_send = jnp.where(leaving_head, head_part, zero_value)
    tail_send = jnp.where(leaving_tail, tail_part, zero_value)
    from_behind = from_behind_2(head_send, "gz", -1)
    from_ahead = from_behind_2(tail_send, "gz", 1)
    head_kept = jnp.where(leaving_head, zero_value, head_part)
    tail_kept = jnp.where(leaving_tail, zero_value, tail_part)
    middle_part = moved_all[:, capacity:tail_start]
    particles_out = jnp.concatenate(
        [from_behind, head_kept, middle_part, tail_kept, from_ahead], axis=1
    )
    return (wake_kick, particles_out)


def solution(mesh):
    return jax.shard_map(
        body,
        mesh=mesh,
        in_specs=(P(None, ("gz", "pa")), P(("gz", "pa")), P("gz", "pa", None), P(), P(), P()),
        out_specs=(P(None, "gz"), P(None, ("gz", "pa"))),
        check_vma=False,
    )
```

profile of v0, /device:TPU:16, one launch (start us, length us, event | category | flops | bytes accessed | tf_op | source)
XLA Modules:
  0.0 447.7 jit_solution(7515340950392063301)
XLA Ops:
  0.6 0.9 broadcast_multiply_fusion.1
  2.4 11.5 %scatter_custom_fusion = f32[3,128]{0,1:T(8,128)S(1)} fusion(s32[2048]{0:T(1024)S(1)} %copy-done.1, f32[2048,3]{1,0:T(8,128)S(1)} %copy.80, f32[]{:T(128)} %constant.22.clone.1), kind=kCustom, calls=%fused_computation.37 | custom fusion | flops 6144 | bytes 1540 | tf_op jit(solution)/shard_map/vmap()/scatter-add | solution.py:121
  14.0 99.1 %psum.7 = f32[3,128]{0,1:T(8,128)S(1)} all-reduce(f32[3,128]{0,1:T(8,128)S(1)} %scatter_custom_fusion), channel_id=1, replica_groups=mesh['gz'=16,'pa'=32] {'pa'}, use_global_device_ids=true, to_apply=%region_1.0 | all-reduce | flops 384 | bytes 3072 | tf_op jit(solution)/shard_map/psum | solution.py:184
  113.9 114.3 %while.11 = (s32[]{:T(128)}, f32[2,8,3]{1,0,2:T(2,128)S(1)}, f32[2,8,3]{1,0,2:T(2,128)S(1)}, f32[8]{0:T(128)S(1)}, f32[8]{0:T(128)S(1)}, /*index=5*/s32[]{:T(128)}) while((s32[]{:T(128)}, f32[2,8,3]{1,0,2:T(2,128)S(1)}, f32[2,8,3]{1,0,2:T(2,128)S(1)}, f32[8]{0:T(128)S(1)}, f32[8]{0:T(128)S(1)}, /*index=5*/s32[]{:T(128)}) %tuple.64), condition=%wide.region_5.7_spmd.clone, body=%wide.region_4.6_spmd.clone.sunk | while | flops 242 | bytes 1901 | solution.py:172
  113.9 3.4 collective-permute-start
  117.4 4.2 collective-permute-done
  121.6 1.9 collective-permute-start
  123.5 5.7 %collective-permute-done = f32[2,8,3]{1,0,2:T(2,128)S(1)} collective-permute-done((f32[2,8,3]{1,0,2:T(2,128)S(1)}, f32[2,8,3]{1,0,2:T(2,128)S(1)}, u32[]{:S(2)}, u32[]{:S(2)}) %collective-permute-start) | collective-permute-done | bytes 224 | tf_op jit(solution)/shard_map/while/body/eval_jaxpr/ppermute | solution.py:25
  129.2 1.9 collective-permute-start
  131.1 5.7 %collective-permute-done = f32[2,8,3]{1,0,2:T(2,128)S(1)} collective-permute-done((f32[2,8,3]{1,0,2:T(2,128)S(1)}, f32[2,8,3]{1,0,2:T(2,128)S(1)}, u32[]{:S(2)}, u32[]{:S(2)}) %collective-permute-start) | collective-permute-done | bytes 224 | tf_op jit(solution)/shard_map/while/body/eval_jaxpr/ppermute | solution.py:25
  136.8 1.9 collective-permute-start
  138.7 5.7 %collective-permute-done = f32[2,8,3]{1,0,2:T(2,128)S(1)} collective-permute-done((f32[2,8,3]{1,0,2:T(2,128)S(1)}, f32[2,8,3]{1,0,2:T(2,128)S(1)}, u32[]{:S(2)}, u32[]{:S(2)}) %collective-permute-start) | collective-permute-done | bytes 224 | tf_op jit(solution)/shard_map/while/body/eval_jaxpr/ppermute | solution.py:25
  144.4 1.9 collective-permute-start
  146.4 5.7 %collective-permute-done = f32[2,8,3]{1,0,2:T(2,128)S(1)} collective-permute-done((f32[2,8,3]{1,0,2:T(2,128)S(1)}, f32[2,8,3]{1,0,2:T(2,128)S(1)}, u32[]{:S(2)}, u32[]{:S(2)}) %collective-permute-start) | collective-permute-done | bytes 224 | tf_op jit(solution)/shard_map/while/body/eval_jaxpr/ppermute | solution.py:25
  152.0 1.9 collective-permute-start
  154.0 5.7 %collective-permute-done = f32[2,8,3]{1,0,2:T(2,128)S(1)} collective-permute-done((f32[2,8,3]{1,0,2:T(2,128)S(1)}, f32[2,8,3]{1,0,2:T(2,128)S(1)}, u32[]{:S(2)}, u32[]{:S(2)}) %collective-permute-start) | collective-permute-done | bytes 224 | tf_op jit(solution)/shard_map/while/body/eval_jaxpr/ppermute | solution.py:25
  159.7 1.9 collective-permute-start
  161.6 5.7 %collective-permute-done = f32[2,8,3]{1,0,2:T(2,128)S(1)} collective-permute-done((f32[2,8,3]{1,0,2:T(2,128)S(1)}, f32[2,8,3]{1,0,2:T(2,128)S(1)}, u32[]{:S(2)}, u32[]{:S(2)}) %collective-permute-start) | collective-permute-done | bytes 224 | tf_op jit(solution)/shard_map/while/body/eval_jaxpr/ppermute | solution.py:25
  167.3 1.9 collective-permute-start
  169.2 5.7 %collective-permute-done = f32[2,8,3]{1,0,2:T(2,128)S(1)} collective-permute-done((f32[2,8,3]{1,0,2:T(2,128)S(1)}, f32[2,8,3]{1,0,2:T(2,128)S(1)}, u32[]{:S(2)}, u32[]{:S(2)}) %collective-permute-start) | collective-permute-done | bytes 224 | tf_op jit(solution)/shard_map/while/body/eval_jaxpr/ppermute | solution.py:25
  174.9 1.9 collective-permute-start
  176.8 5.7 %collective-permute-done = f32[2,8,3]{1,0,2:T(2,128)S(1)} collective-permute-done((f32[2,8,3]{1,0,2:T(2,128)S(1)}, f32[2,8,3]{1,0,2:T(2,128)S(1)}, u32[]{:S(2)}, u32[]{:S(2)}) %collective-permute-start) | collective-permute-done | bytes 224 | tf_op jit(solution)/shard_map/while/body/eval_jaxpr/ppermute | solution.py:25
  182.5 1.9 collective-permute-start
  184.5 5.7 %collective-permute-done = f32[2,8,3]{1,0,2:T(2,128)S(1)} collective-permute-done((f32[2,8,3]{1,0,2:T(2,128)S(1)}, f32[2,8,3]{1,0,2:T(2,128)S(1)}, u32[]{:S(2)}, u32[]{:S(2)}) %collective-permute-start) | collective-permute-done | bytes 224 | tf_op jit(solution)/shard_map/while/body/eval_jaxpr/ppermute | solution.py:25
  190.2 1.9 collective-permute-start
  192.1 5.7 %collective-permute-done = f32[2,8,3]{1,0,2:T(2,128)S(1)} collective-permute-done((f32[2,8,3]{1,0,2:T(2,128)S(1)}, f32[2,8,3]{1,0,2:T(2,128)S(1)}, u32[]{:S(2)}, u32[]{:S(2)}) %collective-permute-start) | collective-permute-done | bytes 224 | tf_op jit(solution)/shard_map/while/body/eval_jaxpr/ppermute | solution.py:25
  197.8 1.9 collective-permute-start
  199.7 5.7 %collective-permute-done = f32[2,8,3]{1,0,2:T(2,128)S(1)} collective-permute-done((f32[2,8,3]{1,0,2:T(2,128)S(1)}, f32[2,8,3]{1,0,2:T(2,128)S(1)}, u32[]{:S(2)}, u32[]{:S(2)}) %collective-permute-start) | collective-permute-done | bytes 224 | tf_op jit(solution)/shard_map/while/body/eval_jaxpr/ppermute | solution.py:25
  205.4 1.9 collective-permute-start
  207.3 5.7 %collective-permute-done = f32[2,8,3]{1,0,2:T(2,128)S(1)} collective-permute-done((f32[2,8,3]{1,0,2:T(2,128)S(1)}, f32[2,8,3]{1,0,2:T(2,128)S(1)}, u32[]{:S(2)}, u32[]{:S(2)}) %collective-permute-start) | collective-permute-done | bytes 224 | tf_op jit(solution)/shard_map/while/body/eval_jaxpr/ppermute | solution.py:25
  213.0 1.9 collective-permute-start
  214.9 5.7 %collective-permute-done = f32[2,8,3]{1,0,2:T(2,128)S(1)} collective-permute-done((f32[2,8,3]{1,0,2:T(2,128)S(1)}, f32[2,8,3]{1,0,2:T(2,128)S(1)}, u32[]{:S(2)}, u32[]{:S(2)}) %collective-permute-start) | collective-permute-done | bytes 224 | tf_op jit(solution)/shard_map/while/body/eval_jaxpr/ppermute | solution.py:25
  220.6 1.9 collective-permute-start
  222.6 5.7 %collective-permute-done = f32[2,8,3]{1,0,2:T(2,128)S(1)} collective-permute-done((f32[2,8,3]{1,0,2:T(2,128)S(1)}, f32[2,8,3]{1,0,2:T(2,128)S(1)}, u32[]{:S(2)}, u32[]{:S(2)}) %collective-permute-start) | collective-permute-done | bytes 224 | tf_op jit(solution)/shard_map/while/body/eval_jaxpr/ppermute | solution.py:25
  228.4 97.2 %gather_fusion.1 = f32[16384]{0:T(1024)S(1)} fusion(f32[128]{0:T(128)S(1)} %get-tuple-element.75, s32[16384]{0:T(1024)S(1)} %bitcast_clamp_fusion), kind=kCustom, calls=%fused_computation.clone | custom fusion | bytes 196608 | tf_op jit(solution)/shard_map/jit(_take)/gather | solution.py:45
  325.8 97.2 %gather_fusion.2 = f32[16384]{0:T(1024)S(1)} fusion(f32[128]{0:T(128)S(1)} %get-tuple-element.76, s32[16384]{0:T(1024)S(1)} %bitcast_clamp_fusion), kind=kCustom, calls=%fused_computation.1.clone | custom fusion | bytes 196608 | tf_op jit(solution)/shard_map/jit(_take)/gather | solution.py:45
  423.8 0.5 copy-done.3
  424.3 5.5 %gather_fusion = f32[2048,3]{1,0:T(8,128)S(1)} fusion(f32[3,128]{0,1:T(8,128)S(1)} %copy.82, s32[2048]{0:T(1024)S(1)} %fusion.32), kind=kCustom, calls=%fused_computation.2 | custom fusion | bytes 57344 | tf_op jit(solution)/shard_map/jit(_take)/gather | solution.py:187
  430.1 0.8 copy-done
  431.0 0.5 multiply_subtract_fusion.1
  431.6 0.6 fusion.68
  432.2 0.7 iota_compare_fusion.1
  432.9 0.5 multiply_subtract_fusion.3
  433.7 1.9 collective-permute-start.1
  436.3 3.0 collective-permute-done.1
  439.4 1.9 collective-permute-start.2
  441.3 5.8 %collective-permute-done.2 = f32[6,384]{1,0:T(8,128)S(1)} collective-permute-done((f32[6,384]{1,0:T(8,128)S(1)}, f32[6,384]{1,0:T(8,128)S(1)}, u32[]{:S(2)}, u32[]{:S(2)}) %collective-permute-start.2) | collective-permute-done | bytes 9248 | tf_op jit(solution)/shard_map/ppermute | solution.py:25
  447.1 0.6 copy-done.5
  (77 shorter events, 4.0 us)
Async XLA Ops:
  1.7 0.7 copy-start.1
  13.9 99.1 %copy-start.2 = (f32[4,8]{1,0:T(4,128)S(1)}, f32[4,8]{1,0:T(4,128)}, u32[]{:S(2)}) copy-start(f32[4,8]{1,0:T(4,128)} %param.15) | copy-start | bytes 388
  13.9 99.1 %copy-start.6 = (f32[8]{0:T(128)S(1)}, f32[8]{0:T(128)}, u32[]{:S(2)}) copy-start(f32[8]{0:T(128)} %param.13) | copy-start | bytes 100
  13.9 99.1 %copy-start.7 = (f32[8]{0:T(128)S(1)}, f32[8]{0:T(128)}, u32[]{:S(2)}) copy-start(f32[8]{0:T(128)} %param.14) | copy-start | bytes 100
  113.9 7.6 %collective-permute-start = (f32[2,8,3]{1,0,2:T(2,128)S(1)}, f32[2,8,3]{1,0,2:T(2,128)S(1)}, u32[]{:S(2)}, u32[]{:S(2)}) collective-permute-start(f32[2,8,3]{1,0,2:T(2,128)S(1)} %maximum_add_fusion.2), channel_id=1, source_target_pairs={{0,32},{32,64},{64,96},{96,128},{128,160},{160,192},{192,224},{224... | collective-permute-start | bytes 584 | tf_op jit(solution)/shard_map/while/body/eval_jaxpr/ppermute | solution.py:25
  121.6 7.6 %collective-permute-start = (f32[2,8,3]{1,0,2:T(2,128)S(1)}, f32[2,8,3]{1,0,2:T(2,128)S(1)}, u32[]{:S(2)}, u32[]{:S(2)}) collective-permute-start(f32[2,8,3]{1,0,2:T(2,128)S(1)} %maximum_add_fusion.2), channel_id=1, source_target_pairs={{0,32},{32,64},{64,96},{96,128},{128,160},{160,192},{192,224},{224... | collective-permute-start | bytes 584 | tf_op jit(solution)/shard_map/while/body/eval_jaxpr/ppermute | solution.py:25
  129.2 7.6 %collective-permute-start = (f32[2,8,3]{1,0,2:T(2,128)S(1)}, f32[2,8,3]{1,0,2:T(2,128)S(1)}, u32[]{:S(2)}, u32[]{:S(2)}) collective-permute-start(f32[2,8,3]{1,0,2:T(2,128)S(1)} %maximum_add_fusion.2), channel_id=1, source_target_pairs={{0,32},{32,64},{64,96},{96,128},{128,160},{160,192},{192,224},{224... | collective-permute-start | bytes 584 | tf_op jit(solution)/shard_map/while/body/eval_jaxpr/ppermute | solution.py:25
  136.8 7.6 %collective-permute-start = (f32[2,8,3]{1,0,2:T(2,128)S(1)}, f32[2,8,3]{1,0,2:T(2,128)S(1)}, u32[]{:S(2)}, u32[]{:S(2)}) collective-permute-start(f32[2,8,3]{1,0,2:T(2,128)S(1)} %maximum_add_fusion.2), channel_id=1, source_target_pairs={{0,32},{32,64},{64,96},{96,128},{128,160},{160,192},{192,224},{224... | collective-permute-start | bytes 584 | tf_op jit(solution)/shard_map/while/body/eval_jaxpr/ppermute | solution.py:25
  144.4 7.6 %collective-permute-start = (f32[2,8,3]{1,0,2:T(2,128)S(1)}, f32[2,8,3]{1,0,2:T(2,128)S(1)}, u32[]{:S(2)}, u32[]{:S(2)}) collective-permute-start(f32[2,8,3]{1,0,2:T(2,128)S(1)} %maximum_add_fusion.2), channel_id=1, source_target_pairs={{0,32},{32,64},{64,96},{96,128},{128,160},{160,192},{192,224},{224... | collective-permute-start | bytes 584 | tf_op jit(solution)/shard_map/while/body/eval_jaxpr/ppermute | solution.py:25
  152.0 7.6 %collective-permute-start = (f32[2,8,3]{1,0,2:T(2,128)S(1)}, f32[2,8,3]{1,0,2:T(2,128)S(1)}, u32[]{:S(2)}, u32[]{:S(2)}) collective-permute-start(f32[2,8,3]{1,0,2:T(2,128)S(1)} %maximum_add_fusion.2), channel_id=1, source_target_pairs={{0,32},{32,64},{64,96},{96,128},{128,160},{160,192},{192,224},{224... | collective-permute-start | bytes 584 | tf_op jit(solution)/shard_map/while/body/eval_jaxpr/ppermute | solution.py:25
  159.7 7.6 %collective-permute-start = (f32[2,8,3]{1,0,2:T(2,128)S(1)}, f32[2,8,3]{1,0,2:T(2,128)S(1)}, u32[]{:S(2)}, u32[]{:S(2)}) collective-permute-start(f32[2,8,3]{1,0,2:T(2,128)S(1)} %maximum_add_fusion.2), channel_id=1, source_target_pairs={{0,32},{32,64},{64,96},{96,128},{128,160},{160,192},{192,224},{224... | collective-permute-start | bytes 584 | tf_op jit(solution)/shard_map/while/body/eval_jaxpr/ppermute | solution.py:25
  167.3 7.6 %collective-permute-start = (f32[2,8,3]{1,0,2:T(2,128)S(1)}, f32[2,8,3]{1,0,2:T(2,128)S(1)}, u32[]{:S(2)}, u32[]{:S(2)}) collective-permute-start(f32[2,8,3]{1,0,2:T(2,128)S(1)} %maximum_add_fusion.2), channel_id=1, source_target_pairs={{0,32},{32,64},{64,96},{96,128},{128,160},{160,192},{192,224},{224... | collective-permute-start | bytes 584 | tf_op jit(solution)/shard_map/while/body/eval_jaxpr/ppermute | solution.py:25
  174.9 7.6 %collective-permute-start = (f32[2,8,3]{1,0,2:T(2,128)S(1)}, f32[2,8,3]{1,0,2:T(2,128)S(1)}, u32[]{:S(2)}, u32[]{:S(2)}) collective-permute-start(f32[2,8,3]{1,0,2:T(2,128)S(1)} %maximum_add_fusion.2), channel_id=1, source_target_pairs={{0,32},{32,64},{64,96},{96,128},{128,160},{160,192},{192,224},{224... | collective-permute-start | bytes 584 | tf_op jit(solution)/shard_map/while/body/eval_jaxpr/ppermute | solution.py:25
  182.5 7.6 %collective-permute-start = (f32[2,8,3]{1,0,2:T(2,128)S(1)}, f32[2,8,3]{1,0,2:T(2,128)S(1)}, u32[]{:S(2)}, u32[]{:S(2)}) collective-permute-start(f32[2,8,3]{1,0,2:T(2,128)S(1)} %maximum_add_fusion.2), channel_id=1, source_target_pairs={{0,32},{32,64},{64,96},{96,128},{128,160},{160,192},{192,224},{224... | collective-permute-start | bytes 584 | tf_op jit(solution)/shard_map/while/body/eval_jaxpr/ppermute | solution.py:25
  190.2 7.6 %collective-permute-start = (f32[2,8,3]{1,0,2:T(2,128)S(1)}, f32[2,8,3]{1,0,2:T(2,128)S(1)}, u32[]{:S(2)}, u32[]{:S(2)}) collective-permute-start(f32[2,8,3]{1,0,2:T(2,128)S(1)} %maximum_add_fusion.2), channel_id=1, source_target_pairs={{0,32},{32,64},{64,96},{96,128},{128,160},{160,192},{192,224},{224... | collective-permute-start | bytes 584 | tf_op jit(solution)/shard_map/while/body/eval_jaxpr/ppermute | solution.py:25
  197.8 7.6 %collective-permute-start = (f32[2,8,3]{1,0,2:T(2,128)S(1)}, f32[2,8,3]{1,0,2:T(2,128)S(1)}, u32[]{:S(2)}, u32[]{:S(2)}) collective-permute-start(f32[2,8,3]{1,0,2:T(2,128)S(1)} %maximum_add_fusion.2), channel_id=1, source_target_pairs={{0,32},{32,64},{64,96},{96,128},{128,160},{160,192},{192,224},{224... | collective-permute-start | bytes 584 | tf_op jit(solution)/shard_map/while/body/eval_jaxpr/ppermute | solution.py:25
  205.4 7.6 %collective-permute-start = (f32[2,8,3]{1,0,2:T(2,128)S(1)}, f32[2,8,3]{1,0,2:T(2,128)S(1)}, u32[]{:S(2)}, u32[]{:S(2)}) collective-permute-start(f32[2,8,3]{1,0,2:T(2,128)S(1)} %maximum_add_fusion.2), channel_id=1, source_target_pairs={{0,32},{32,64},{64,96},{96,128},{128,160},{160,192},{192,224},{224... | collective-permute-start | bytes 584 | tf_op jit(solution)/shard_map/while/body/eval_jaxpr/ppermute | solution.py:25
  213.0 7.6 %collective-permute-start = (f32[2,8,3]{1,0,2:T(2,128)S(1)}, f32[2,8,3]{1,0,2:T(2,128)S(1)}, u32[]{:S(2)}, u32[]{:S(2)}) collective-permute-start(f32[2,8,3]{1,0,2:T(2,128)S(1)} %maximum_add_fusion.2), channel_id=1, source_target_pairs={{0,32},{32,64},{64,96},{96,128},{128,160},{160,192},{192,224},{224... | collective-permute-start | bytes 584 | tf_op jit(solution)/shard_map/while/body/eval_jaxpr/ppermute | solution.py:25
  220.6 7.6 %collective-permute-start = (f32[2,8,3]{1,0,2:T(2,128)S(1)}, f32[2,8,3]{1,0,2:T(2,128)S(1)}, u32[]{:S(2)}, u32[]{:S(2)}) collective-permute-start(f32[2,8,3]{1,0,2:T(2,128)S(1)} %maximum_add_fusion.2), channel_id=1, source_target_pairs={{0,32},{32,64},{64,96},{96,128},{128,160},{160,192},{192,224},{224... | collective-permute-start | bytes 584 | tf_op jit(solution)/shard_map/while/body/eval_jaxpr/ppermute | solution.py:25
  423.7 0.6 copy-start.3
  430.1 0.9 copy-start
  431.0 0.7 copy-start.4
  433.7 5.6 %collective-permute-start.1 = (f32[6,384]{1,0:T(8,128)S(1)}, f32[6,384]{1,0:T(8,128)S(1)}, u32[]{:S(2)}, u32[]{:S(2)}) collective-permute-start(f32[6,384]{1,0:T(8,128)S(1)} %slice_select_fusion.1), channel_id=1, source_target_pairs={{32,0},{64,32},{96,64},{128,96},{160,128},{192,160},{224,192},{256... | collective-permute-start | bytes 27656 | tf_op jit(solution)/shard_map/ppermute | solution.py:25
  439.4 7.7 %collective-permute-start.2 = (f32[6,384]{1,0:T(8,128)S(1)}, f32[6,384]{1,0:T(8,128)S(1)}, u32[]{:S(2)}, u32[]{:S(2)}) collective-permute-start(f32[6,384]{1,0:T(8,128)S(1)} %get-tuple-element.109), channel_id=1, source_target_pairs={{0,32},{32,64},{64,96},{96,128},{128,160},{160,192},{192,224},{224... | collective-permute-start | bytes 27656 | tf_op jit(solution)/shard_map/ppermute | solution.py:25
  447.1 0.6 copy-start.5
where the time goes:
time: 450 us; the launch traced here: 448 us
  local copies, waits for them, and re-layouts  204 us (45%)
  blocking collectives  99.1 us (22%)
  waiting for transfers between devices  92.3 us (21%)
  starting transfers between devices  34.1 us (8%)
  other arithmetic  15 us (3%)
    gather x2, local copies, waits for them, and re-layouts, toeplitz(): picked = jnp.take(wave, jnp.clip(offset, 0, slab_width - 1))  194 us
    psum x1, blocking collectives, body(): moments = lax.psum(partial_moments, 'pa')  99.1 us
    ppermute x17, waiting for transfers between devices, from_behind_2(): lax.ppermute(value, axis, [(source, source + steps) for source in range(l...  92.3 us
    ppermute x17, starting transfers between devices, from_behind_2(): lax.ppermute(value, axis, [(source, source + steps) for source in range(l...  34.1 us
    scatter-add x1, other arithmetic, deposit(): jax.ops.segment_sum(column, index, num_segments=segments)  11.5 us
  transfers between devices with their start and end apart: 17, of which 17 were waited for; matrix products, arithmetic and copies ran while one was open for 0% of the time, Pallas kernels for 0%

commit v1 on v0

--- a/solution.py
+++ b/solution.py
@@ -181,7 +181,7 @@
     mean_fill = local_count * member_count / slab_width
     values = moment_values(particles, mean_fill)
     partial_moments = deposit(values, slice_index, slab_width)
-    moments = lax.psum(partial_moments, "pa")
+    moments = jnp.sum(lax.all_gather(partial_moments, "pa"), axis=0)
     carried = upstream(slab_summary(moments, tables), tables[6], slab_count)
     wake_kick = slab_kick(moments, carried, tables)
     per_particle = jnp.take(wake_kick, slice_index, axis=1)

time: 450 us -> 388 us (0.86)
  blocking collectives: 99.1 us -> 36.4 us
    psum x1 -> x0, blocking collectives: 99.1 us -> none  [body(): moments = lax.psum(partial_moments, 'pa')]
    all_gather x0 -> x1, blocking collectives: none -> 36.4 us  [body(): moments = jnp.sum(lax.all_gather(partial_moments, 'pa'), axis=0)]
where the time goes in v1:
time: 388 us; the launch traced here: 385 us
  local copies, waits for them, and re-layouts  205 us (53%)
  waiting for transfers between devices  92.3 us (24%)
  blocking collectives  36.4 us (9%)
  starting transfers between devices  34.1 us (9%)
  other arithmetic  15.1 us (4%)
    gather x2, local copies, waits for them, and re-layouts, toeplitz(): picked = jnp.take(wave, jnp.clip(offset, 0, slab_width - 1))  194 us
    ppermute x17, waiting for transfers between devices, from_behind_2(): lax.ppermute(value, axis, [(source, source + steps) for source in range(l...  92.3 us
    all_gather x1, blocking collectives, body(): moments = jnp.sum(lax.all_gather(partial_moments, 'pa'), axis=0)  36.4 us
    ppermute x17, starting transfers between devices, from_behind_2(): lax.ppermute(value, axis, [(source, source + steps) for source in range(l...  34.1 us
    scatter-add x1, other arithmetic, deposit(): jax.ops.segment_sum(column, index, num_segments=segments)  11.5 us
  transfers between devices with their start and end apart: 17, of which 17 were waited for; matrix products, arithmetic and copies ran while one was open for 0% of the time, Pallas kernels for 0%

profile of v1, /device:TPU:16, one launch (start us, length us, event | category | flops | bytes accessed | tf_op | source)
XLA Modules:
  0.0 385.5 jit_solution(815268996868322272)
XLA Ops:
  0.6 0.9 broadcast_multiply_fusion.1
  2.4 11.5 %scatter_custom_fusion = f32[3,128]{0,1:T(8,128)S(1)} fusion(s32[2048]{0:T(1024)S(1)} %copy-done.1, f32[2048,3]{1,0:T(8,128)S(1)} %copy.109, f32[]{:T(128)} %constant.22.clone.1), kind=kCustom, calls=%fused_computation.35 | custom fusion | flops 6144 | bytes 1540 | tf_op jit(solution)/shard_map/vmap()/scatter-add | solution.py:121
  14.0 36.4 %all-gather.1 = f32[32,3,128]{2,1,0:T(4,128)S(1)} all-gather(f32[1,3,128]{2,1,0:T(4,128)S(1)} %copy.110), channel_id=2, replica_groups=mesh['gz'=16,'pa'=32] {'pa'}, dimensions={0}, use_global_device_ids=true | all-gather | bytes 50688 | tf_op jit(solution)/shard_map/all_gather | solution.py:184
  50.4 0.6 copy-done.2
  51.7 114.3 %while.11 = (s32[]{:T(128)}, f32[2,8,3]{1,0,2:T(2,128)S(1)}, f32[2,8,3]{1,0,2:T(2,128)S(1)}, f32[8]{0:T(128)S(1)}, f32[8]{0:T(128)S(1)}, /*index=5*/s32[]{:T(128)}) while((s32[]{:T(128)}, f32[2,8,3]{1,0,2:T(2,128)S(1)}, f32[2,8,3]{1,0,2:T(2,128)S(1)}, f32[8]{0:T(128)S(1)}, f32[8]{0:T(128)S(1)}, /*index=5*/s32[]{:T(128)}) %tuple.65), condition=%wide.region_5.7_spmd.clone, body=%wide.region_4.6_spmd.clone.sunk | while | flops 242 | bytes 1901 | solution.py:172
  51.8 3.4 collective-permute-start
  55.2 4.2 %collective-permute-done = f32[2,8,3]{1,0,2:T(2,128)S(1)} collective-permute-done((f32[2,8,3]{1,0,2:T(2,128)S(1)}, f32[2,8,3]{1,0,2:T(2,128)S(1)}, u32[]{:S(2)}, u32[]{:S(2)}) %collective-permute-start) | collective-permute-done | bytes 224 | tf_op jit(solution)/shard_map/while/body/eval_jaxpr/ppermute | solution.py:25
  59.4 1.9 collective-permute-start
  61.3 5.7 %collective-permute-done = f32[2,8,3]{1,0,2:T(2,128)S(1)} collective-permute-done((f32[2,8,3]{1,0,2:T(2,128)S(1)}, f32[2,8,3]{1,0,2:T(2,128)S(1)}, u32[]{:S(2)}, u32[]{:S(2)}) %collective-permute-start) | collective-permute-done | bytes 224 | tf_op jit(solution)/shard_map/while/body/eval_jaxpr/ppermute | solution.py:25
  67.0 1.9 collective-permute-start
  69.0 5.7 %collective-permute-done = f32[2,8,3]{1,0,2:T(2,128)S(1)} collective-permute-done((f32[2,8,3]{1,0,2:T(2,128)S(1)}, f32[2,8,3]{1,0,2:T(2,128)S(1)}, u32[]{:S(2)}, u32[]{:S(2)}) %collective-permute-start) | collective-permute-done | bytes 224 | tf_op jit(solution)/shard_map/while/body/eval_jaxpr/ppermute | solution.py:25
  74.7 1.9 collective-permute-start
  76.6 5.7 %collective-permute-done = f32[2,8,3]{1,0,2:T(2,128)S(1)} collective-permute-done((f32[2,8,3]{1,0,2:T(2,128)S(1)}, f32[2,8,3]{1,0,2:T(2,128)S(1)}, u32[]{:S(2)}, u32[]{:S(2)}) %collective-permute-start) | collective-permute-done | bytes 224 | tf_op jit(solution)/shard_map/while/body/eval_jaxpr/ppermute | solution.py:25
  82.3 1.9 collective-permute-start
  84.2 5.7 %collective-permute-done = f32[2,8,3]{1,0,2:T(2,128)S(1)} collective-permute-done((f32[2,8,3]{1,0,2:T(2,128)S(1)}, f32[2,8,3]{1,0,2:T(2,128)S(1)}, u32[]{:S(2)}, u32[]{:S(2)}) %collective-permute-start) | collective-permute-done | bytes 224 | tf_op jit(solution)/shard_map/while/body/eval_jaxpr/ppermute | solution.py:25
  89.9 1.9 collective-permute-start
  91.8 5.7 %collective-permute-done = f32[2,8,3]{1,0,2:T(2,128)S(1)} collective-permute-done((f32[2,8,3]{1,0,2:T(2,128)S(1)}, f32[2,8,3]{1,0,2:T(2,128)S(1)}, u32[]{:S(2)}, u32[]{:S(2)}) %collective-permute-start) | collective-permute-done | bytes 224 | tf_op jit(solution)/shard_map/while/body/eval_jaxpr/ppermute | solution.py:25
  97.5 1.9 collective-permute-start
  99.4 5.7 %collective-permute-done = f32[2,8,3]{1,0,2:T(2,128)S(1)} collective-permute-done((f32[2,8,3]{1,0,2:T(2,128)S(1)}, f32[2,8,3]{1,0,2:T(2,128)S(1)}, u32[]{:S(2)}, u32[]{:S(2)}) %collective-permute-start) | collective-permute-done | bytes 224 | tf_op jit(solution)/shard_map/while/body/eval_jaxpr/ppermute | solution.py:25
  105.1 1.9 collective-permute-start
  107.1 5.7 %collective-permute-done = f32[2,8,3]{1,0,2:T(2,128)S(1)} collective-permute-done((f32[2,8,3]{1,0,2:T(2,128)S(1)}, f32[2,8,3]{1,0,2:T(2,128)S(1)}, u32[]{:S(2)}, u32[]{:S(2)}) %collective-permute-start) | collective-permute-done | bytes 224 | tf_op jit(solution)/shard_map/while/body/eval_jaxpr/ppermute | solution.py:25
  112.8 1.9 collective-permute-start
  114.7 5.7 %collective-permute-done = f32[2,8,3]{1,0,2:T(2,128)S(1)} collective-permute-done((f32[2,8,3]{1,0,2:T(2,128)S(1)}, f32[2,8,3]{1,0,2:T(2,128)S(1)}, u32[]{:S(2)}, u32[]{:S(2)}) %collective-permute-start) | collective-permute-done | bytes 224 | tf_op jit(solution)/shard_map/while/body/eval_jaxpr/ppermute | solution.py:25
  120.4 1.9 collective-permute-start
  122.3 5.7 %collective-permute-done = f32[2,8,3]{1,0,2:T(2,128)S(1)} collective-permute-done((f32[2,8,3]{1,0,2:T(2,128)S(1)}, f32[2,8,3]{1,0,2:T(2,128)S(1)}, u32[]{:S(2)}, u32[]{:S(2)}) %collective-permute-start) | collective-permute-done | bytes 224 | tf_op jit(solution)/shard_map/while/body/eval_jaxpr/ppermute | solution.py:25
  128.0 1.9 collective-permute-start
  129.9 5.7 %collective-permute-done = f32[2,8,3]{1,0,2:T(2,128)S(1)} collective-permute-done((f32[2,8,3]{1,0,2:T(2,128)S(1)}, f32[2,8,3]{1,0,2:T(2,128)S(1)}, u32[]{:S(2)}, u32[]{:S(2)}) %collective-permute-start) | collective-permute-done | bytes 224 | tf_op jit(solution)/shard_map/while/body/eval_jaxpr/ppermute | solution.py:25
  135.6 1.9 collective-permute-start
  137.5 5.7 %collective-permute-done = f32[2,8,3]{1,0,2:T(2,128)S(1)} collective-permute-done((f32[2,8,3]{1,0,2:T(2,128)S(1)}, f32[2,8,3]{1,0,2:T(2,128)S(1)}, u32[]{:S(2)}, u32[]{:S(2)}) %collective-permute-start) | collective-permute-done | bytes 224 | tf_op jit(solution)/shard_map/while/body/eval_jaxpr/ppermute | solution.py:25
  143.2 1.9 collective-permute-start
  145.2 5.7 %collective-permute-done = f32[2,8,3]{1,0,2:T(2,128)S(1)} collective-permute-done((f32[2,8,3]{1,0,2:T(2,128)S(1)}, f32[2,8,3]{1,0,2:T(2,128)S(1)}, u32[]{:S(2)}, u32[]{:S(2)}) %collective-permute-start) | collective-permute-done | bytes 224 | tf_op jit(solution)/shard_map/while/body/eval_jaxpr/ppermute | solution.py:25
  150.9 1.9 collective-permute-start
  152.8 5.7 %collective-permute-done = f32[2,8,3]{1,0,2:T(2,128)S(1)} collective-permute-done((f32[2,8,3]{1,0,2:T(2,128)S(1)}, f32[2,8,3]{1,0,2:T(2,128)S(1)}, u32[]{:S(2)}, u32[]{:S(2)}) %collective-permute-start) | collective-permute-done | bytes 224 | tf_op jit(solution)/shard_map/while/body/eval_jaxpr/ppermute | solution.py:25
  158.5 1.9 collective-permute-start
  160.4 5.7 %collective-permute-done = f32[2,8,3]{1,0,2:T(2,128)S(1)} collective-permute-done((f32[2,8,3]{1,0,2:T(2,128)S(1)}, f32[2,8,3]{1,0,2:T(2,128)S(1)}, u32[]{:S(2)}, u32[]{:S(2)}) %collective-permute-start) | collective-permute-done | bytes 224 | tf_op jit(solution)/shard_map/while/body/eval_jaxpr/ppermute | solution.py:25
  166.2 97.2 %gather_fusion.2 = f32[16384]{0:T(1024)S(1)} fusion(f32[128]{0:T(128)S(1)} %get-tuple-element.81, s32[16384]{0:T(1024)S(1)} %bitcast_clamp_fusion), kind=kCustom, calls=%fused_computation.1.clone | custom fusion | bytes 196608 | tf_op jit(solution)/shard_map/jit(_take)/gather | solution.py:45
  263.4 97.2 %gather_fusion.1 = f32[16384]{0:T(1024)S(1)} fusion(f32[128]{0:T(128)S(1)} %get-tuple-element.80, s32[16384]{0:T(1024)S(1)} %bitcast_clamp_fusion), kind=kCustom, calls=%fused_computation.clone | custom fusion | bytes 196608 | tf_op jit(solution)/shard_map/jit(_take)/gather | solution.py:45
  362.1 5.5 %gather_fusion = f32[2048,3]{1,0:T(8,128)S(1)} fusion(f32[3,128]{0,1:T(8,128)S(1)} %copy.113, s32[2048]{0:T(1024)S(1)} %fusion.31), kind=kCustom, calls=%fused_computation.2 | custom fusion | bytes 57344 | tf_op jit(solution)/shard_map/jit(_take)/gather | solution.py:187
  367.9 0.8 copy-done
  368.8 0.5 multiply_subtract_fusion.1
  369.4 0.6 fusion.67
  370.0 0.7 iota_compare_fusion.1
  370.7 0.5 multiply_subtract_fusion.3
  371.5 1.9 collective-permute-start.1
  374.1 3.0 collective-permute-done.1
  377.1 1.9 collective-permute-start.2
  379.1 5.8 %collective-permute-done.2 = f32[6,384]{1,0:T(8,128)S(1)} collective-permute-done((f32[6,384]{1,0:T(8,128)S(1)}, f32[6,384]{1,0:T(8,128)S(1)}, u32[]{:S(2)}, u32[]{:S(2)}) %collective-permute-start.2) | collective-permute-done | bytes 9248 | tf_op jit(solution)/shard_map/ppermute | solution.py:25
  384.8 0.6 copy-done.5
  (79 shorter events, 4.3 us)
Async XLA Ops:
  1.7 0.7 copy-start.1
  50.4 0.7 copy-start.2
  50.4 0.7 copy-start.6
  50.4 0.7 copy-start.7
  51.8 7.6 %collective-permute-start = (f32[2,8,3]{1,0,2:T(2,128)S(1)}, f32[2,8,3]{1,0,2:T(2,128)S(1)}, u32[]{:S(2)}, u32[]{:S(2)}) collective-permute-start(f32[2,8,3]{1,0,2:T(2,128)S(1)} %maximum_add_fusion.2), channel_id=1, source_target_pairs={{0,32},{32,64},{64,96},{96,128},{128,160},{160,192},{192,224},{224... | collective-permute-start | bytes 584 | tf_op jit(solution)/shard_map/while/body/eval_jaxpr/ppermute | solution.py:25
  59.4 7.6 %collective-permute-start = (f32[2,8,3]{1,0,2:T(2,128)S(1)}, f32[2,8,3]{1,0,2:T(2,128)S(1)}, u32[]{:S(2)}, u32[]{:S(2)}) collective-permute-start(f32[2,8,3]{1,0,2:T(2,128)S(1)} %maximum_add_fusion.2), channel_id=1, source_target_pairs={{0,32},{32,64},{64,96},{96,128},{128,160},{160,192},{192,224},{224... | collective-permute-start | bytes 584 | tf_op jit(solution)/shard_map/while/body/eval_jaxpr/ppermute | solution.py:25
  67.0 7.6 %collective-permute-start = (f32[2,8,3]{1,0,2:T(2,128)S(1)}, f32[2,8,3]{1,0,2:T(2,128)S(1)}, u32[]{:S(2)}, u32[]{:S(2)}) collective-permute-start(f32[2,8,3]{1,0,2:T(2,128)S(1)} %maximum_add_fusion.2), channel_id=1, source_target_pairs={{0,32},{32,64},{64,96},{96,128},{128,160},{160,192},{192,224},{224... | collective-permute-start | bytes 584 | tf_op jit(solution)/shard_map/while/body/eval_jaxpr/ppermute | solution.py:25
  74.7 7.6 %collective-permute-start = (f32[2,8,3]{1,0,2:T(2,128)S(1)}, f32[2,8,3]{1,0,2:T(2,128)S(1)}, u32[]{:S(2)}, u32[]{:S(2)}) collective-permute-start(f32[2,8,3]{1,0,2:T(2,128)S(1)} %maximum_add_fusion.2), channel_id=1, source_target_pairs={{0,32},{32,64},{64,96},{96,128},{128,160},{160,192},{192,224},{224... | collective-permute-start | bytes 584 | tf_op jit(solution)/shard_map/while/body/eval_jaxpr/ppermute | solution.py:25
  82.3 7.6 %collective-permute-start = (f32[2,8,3]{1,0,2:T(2,128)S(1)}, f32[2,8,3]{1,0,2:T(2,128)S(1)}, u32[]{:S(2)}, u32[]{:S(2)}) collective-permute-start(f32[2,8,3]{1,0,2:T(2,128)S(1)} %maximum_add_fusion.2), channel_id=1, source_target_pairs={{0,32},{32,64},{64,96},{96,128},{128,160},{160,192},{192,224},{224... | collective-permute-start | bytes 584 | tf_op jit(solution)/shard_map/while/body/eval_jaxpr/ppermute | solution.py:25
  89.9 7.6 %collective-permute-start = (f32[2,8,3]{1,0,2:T(2,128)S(1)}, f32[2,8,3]{1,0,2:T(2,128)S(1)}, u32[]{:S(2)}, u32[]{:S(2)}) collective-permute-start(f32[2,8,3]{1,0,2:T(2,128)S(1)} %maximum_add_fusion.2), channel_id=1, source_target_pairs={{0,32},{32,64},{64,96},{96,128},{128,160},{160,192},{192,224},{224... | collective-permute-start | bytes 584 | tf_op jit(solution)/shard_map/while/body/eval_jaxpr/ppermute | solution.py:25
  97.5 7.6 %collective-permute-start = (f32[2,8,3]{1,0,2:T(2,128)S(1)}, f32[2,8,3]{1,0,2:T(2,128)S(1)}, u32[]{:S(2)}, u32[]{:S(2)}) collective-permute-start(f32[2,8,3]{1,0,2:T(2,128)S(1)} %maximum_add_fusion.2), channel_id=1, source_target_pairs={{0,32},{32,64},{64,96},{96,128},{128,160},{160,192},{192,224},{224... | collective-permute-start | bytes 584 | tf_op jit(solution)/shard_map/while/body/eval_jaxpr/ppermute | solution.py:25
  105.1 7.6 %collective-permute-start = (f32[2,8,3]{1,0,2:T(2,128)S(1)}, f32[2,8,3]{1,0,2:T(2,128)S(1)}, u32[]{:S(2)}, u32[]{:S(2)}) collective-permute-start(f32[2,8,3]{1,0,2:T(2,128)S(1)} %maximum_add_fusion.2), channel_id=1, source_target_pairs={{0,32},{32,64},{64,96},{96,128},{128,160},{160,192},{192,224},{224... | collective-permute-start | bytes 584 | tf_op jit(solution)/shard_map/while/body/eval_jaxpr/ppermute | solution.py:25
  112.8 7.6 %collective-permute-start = (f32[2,8,3]{1,0,2:T(2,128)S(1)}, f32[2,8,3]{1,0,2:T(2,128)S(1)}, u32[]{:S(2)}, u32[]{:S(2)}) collective-permute-start(f32[2,8,3]{1,0,2:T(2,128)S(1)} %maximum_add_fusion.2), channel_id=1, source_target_pairs={{0,32},{32,64},{64,96},{96,128},{128,160},{160,192},{192,224},{224... | collective-permute-start | bytes 584 | tf_op jit(solution)/shard_map/while/body/eval_jaxpr/ppermute | solution.py:25
  120.4 7.6 %collective-permute-start = (f32[2,8,3]{1,0,2:T(2,128)S(1)}, f32[2,8,3]{1,0,2:T(2,128)S(1)}, u32[]{:S(2)}, u32[]{:S(2)}) collective-permute-start(f32[2,8,3]{1,0,2:T(2,128)S(1)} %maximum_add_fusion.2), channel_id=1, source_target_pairs={{0,32},{32,64},{64,96},{96,128},{128,160},{160,192},{192,224},{224... | collective-permute-start | bytes 584 | tf_op jit(solution)/shard_map/while/body/eval_jaxpr/ppermute | solution.py:25
  128.0 7.6 %collective-permute-start = (f32[2,8,3]{1,0,2:T(2,128)S(1)}, f32[2,8,3]{1,0,2:T(2,128)S(1)}, u32[]{:S(2)}, u32[]{:S(2)}) collective-permute-start(f32[2,8,3]{1,0,2:T(2,128)S(1)} %maximum_add_fusion.2), channel_id=1, source_target_pairs={{0,32},{32,64},{64,96},{96,128},{128,160},{160,192},{192,224},{224... | collective-permute-start | bytes 584 | tf_op jit(solution)/shard_map/while/body/eval_jaxpr/ppermute | solution.py:25
  135.6 7.6 %collective-permute-start = (f32[2,8,3]{1,0,2:T(2,128)S(1)}, f32[2,8,3]{1,0,2:T(2,128)S(1)}, u32[]{:S(2)}, u32[]{:S(2)}) collective-permute-start(f32[2,8,3]{1,0,2:T(2,128)S(1)} %maximum_add_fusion.2), channel_id=1, source_target_pairs={{0,32},{32,64},{64,96},{96,128},{128,160},{160,192},{192,224},{224... | collective-permute-start | bytes 584 | tf_op jit(solution)/shard_map/while/body/eval_jaxpr/ppermute | solution.py:25
  143.2 7.6 %collective-permute-start = (f32[2,8,3]{1,0,2:T(2,128)S(1)}, f32[2,8,3]{1,0,2:T(2,128)S(1)}, u32[]{:S(2)}, u32[]{:S(2)}) collective-permute-start(f32[2,8,3]{1,0,2:T(2,128)S(1)} %maximum_add_fusion.2), channel_id=1, source_target_pairs={{0,32},{32,64},{64,96},{96,128},{128,160},{160,192},{192,224},{224... | collective-permute-start | bytes 584 | tf_op jit(solution)/shard_map/while/body/eval_jaxpr/ppermute | solution.py:25
  150.9 7.6 %collective-permute-start = (f32[2,8,3]{1,0,2:T(2,128)S(1)}, f32[2,8,3]{1,0,2:T(2,128)S(1)}, u32[]{:S(2)}, u32[]{:S(2)}) collective-permute-start(f32[2,8,3]{1,0,2:T(2,128)S(1)} %maximum_add_fusion.2), channel_id=1, source_target_pairs={{0,32},{32,64},{64,96},{96,128},{128,160},{160,192},{192,224},{224... | collective-permute-start | bytes 584 | tf_op jit(solution)/shard_map/while/body/eval_jaxpr/ppermute | solution.py:25
  158.5 7.6 %collective-permute-start = (f32[2,8,3]{1,0,2:T(2,128)S(1)}, f32[2,8,3]{1,0,2:T(2,128)S(1)}, u32[]{:S(2)}, u32[]{:S(2)}) collective-permute-start(f32[2,8,3]{1,0,2:T(2,128)S(1)} %maximum_add_fusion.2), channel_id=1, source_target_pairs={{0,32},{32,64},{64,96},{96,128},{128,160},{160,192},{192,224},{224... | collective-permute-start | bytes 584 | tf_op jit(solution)/shard_map/while/body/eval_jaxpr/ppermute | solution.py:25
  361.5 0.6 copy-start.3
  367.9 0.9 copy-start
  368.8 0.7 copy-start.4
  371.5 5.6 %collective-permute-start.1 = (f32[6,384]{1,0:T(8,128)S(1)}, f32[6,384]{1,0:T(8,128)S(1)}, u32[]{:S(2)}, u32[]{:S(2)}) collective-permute-start(f32[6,384]{1,0:T(8,128)S(1)} %slice_select_fusion.1), channel_id=1, source_target_pairs={{32,0},{64,32},{96,64},{128,96},{160,128},{192,160},{224,192},{256... | collective-permute-start | bytes 27656 | tf_op jit(solution)/shard_map/ppermute | solution.py:25
  377.1 7.7 %collective-permute-start.2 = (f32[6,384]{1,0:T(8,128)S(1)}, f32[6,384]{1,0:T(8,128)S(1)}, u32[]{:S(2)}, u32[]{:S(2)}) collective-permute-start(f32[6,384]{1,0:T(8,128)S(1)} %get-tuple-element.114), channel_id=1, source_target_pairs={{0,32},{32,64},{64,96},{96,128},{128,160},{160,192},{192,224},{224... | collective-permute-start | bytes 27656 | tf_op jit(solution)/shard_map/ppermute | solution.py:25
  384.8 0.6 copy-start.5
